TPU v7x, 256 devices: a whole 4x4x8 slice. The times are simulated.
256 devices in a mesh: ctx: 64 (over x, z, y_lo), head: 4 (over y_hi, core).
Axes of the slice: x: 4, y: 4 (y_hi: 2, y_lo: 2; y = y_hi * 2 + y_lo), z: 8, core: 2. Of those that a mesh axis runs over, the one named last changes fastest.
Arguments:
- queries: bfloat16 [16384, 2048], P('ctx', 'head'), may hold values from -32 to 32
- key_heads: bfloat16 [16384, 2048], P('ctx', 'head'), may hold values from -32 to 32
- value_heads: bfloat16 [16384, 2048], P('ctx', 'head'), may hold values from -6 to 6
- out_weight: bfloat16 [4096, 2048], P('ctx', 'head'), may hold values from -0.5 to 0.5
- block_lists: int32 [128, 3], replicated, may hold values from 0 to 127, as said below
- out_grad: bfloat16 [16384, 4096], P('ctx', 'head'), may hold values from -16 to 16
Outputs:
- attended: bfloat16 [16384, 4096], P('ctx', 'head')
- query_grad: bfloat16 [16384, 2048], P('ctx', 'head')
- key_grad: bfloat16 [16384, 2048], P('ctx', 'head')
- value_grad: bfloat16 [16384, 2048], P('ctx', 'head')
- weight_grad: float32 [4096, 2048], P('ctx', 'head')
Inputs may be any that keep to these rules, and one draw needn't show every extreme that they name: `block_lists`: every entry of row b lies within 4 blocks of b, and the first entry of each row lies exactly 4 blocks away from b.
All inputs are finite; a program needn't handle non-finite values.
Results may differ from a plain program's by a relative error of at most 0.028.
Values may be sent and summed in bfloat16 or wider, within the bound.
A program may use at most 128 MiB of HBM per device.

v0:
```python
import jax
import jax.numpy as jnp
from jax import lax
from jax.sharding import PartitionSpec as P

HD = 128
BLK = 128
CYCLE = 2


def passed_along(x, axis, by):
    peers = lax.axis_size(axis)
    return lax.ppermute(x, axis, [(i, (i + by) % peers) for i in range(peers)])


def spread(value, axis, source):
    kept = jnp.where(lax.axis_index(axis) == source, value, 0).astype(value.dtype)
    return lax.psum(kept, axis)


def local(queries, key_heads, value_heads, out_weight, block_lists, out_grad):
    head_size = HD
    block = BLK
    reach_runs = CYCLE
    scale = head_size ** (-0.5)
    tok_dev = queries.shape[0]
    features = queries.shape[1]
    groups = features // head_size
    per_dev = tok_dev // block
    total_blocks = per_dev * lax.axis_size("ctx")
    run_index = lax.axis_index("ctx")
    band_count = 2 * reach_runs + 1
    stacked = jnp.stack([key_heads, value_heads])
    moving = passed_along(stacked, "ctx", -reach_runs)
    pieces = [moving]
    for turn in range(2 * reach_runs):
        moving = passed_along(moving, "ctx", 1)
        pieces.append(moving)
    pieces = pieces[::-1]
    band = jnp.stack(pieces)
    first = spread(stacked[:, :block], "ctx", 0)
    band_ids = (run_index - reach_runs) * per_dev + jnp.arange(
        band_count * per_dev, dtype=jnp.int32
    )
    query_ids = run_index * per_dev + jnp.arange(per_dev, dtype=jnp.int32)
    local_lists = lax.dynamic_slice_in_dim(block_lists, run_index * per_dev, per_dev, 0)
    listed = jnp.any(local_lists[:, :, None] == band_ids[None, None, :], axis=1)
    nearby = jnp.abs(band_ids[None, :] - query_ids[:, None]) <= 1
    inside = (band_ids >= 1) & (band_ids < total_blocks)
    allowed = (listed | nearby) & inside[None, :]
    token_mask = jnp.repeat(jnp.repeat(allowed, block, 0), block, 1)
    band_keys = band[:, 0].reshape(band_count * tok_dev, groups, head_size)
    band_values = band[:, 1].reshape(band_count * tok_dev, groups, head_size)
    first_keys = first[0].reshape(block, groups, head_size)
    first_values = first[1].reshape(block, groups, head_size)
    query_view = queries.reshape(tok_dev, groups, head_size)
    band_scores = (
        jnp.einsum("qhd,khd->hqk", query_view, band_keys, preferred_element_type=jnp.float32)
        * scale
    )
    first_scores = (
        jnp.einsum("qhd,khd->hqk", query_view, first_keys, preferred_element_type=jnp.float32)
        * scale
    )
    band_scores = jnp.where(token_mask[None], band_scores, -jnp.inf)
    row_top = jnp.maximum(jnp.max(band_scores, axis=2), jnp.max(first_scores, axis=2))
    band_exp = jnp.exp(band_scores - row_top[:, :, None])
    first_exp = jnp.exp(first_scores - row_top[:, :, None])
    denominator = jnp.sum(band_exp, axis=2) + jnp.sum(first_exp, axis=2)
    band_prob = band_exp / denominator[:, :, None]
    first_prob = first_exp / denominator[:, :, None]
    band_low = band_prob.astype(jnp.bfloat16)
    first_low = first_prob.astype(jnp.bfloat16)
    mixed_heads = jnp.einsum(
        "hqk,khd->qhd", band_low, band_values, preferred_element_type=jnp.float32
    )
    mixed_heads = mixed_heads + jnp.einsum(
        "hqk,khd->qhd", first_low, first_values, preferred_element_type=jnp.float32
    )
    mixed = mixed_heads.reshape(tok_dev, features).astype(jnp.bfloat16)
    contract_last = (((1,), (1,)), ((), ()))
    full_weight = lax.all_gather(out_weight, "ctx", axis=0, tiled=True)
    partial_out = lax.dot_general(
        mixed, full_weight, contract_last, preferred_element_type=jnp.float32
    )
    attended = lax.psum_scatter(
        partial_out.astype(jnp.bfloat16), "head", scatter_dimension=1, tiled=True
    )
    grad_full = lax.all_gather(out_grad, "head", axis=1, tiled=True)
    mixed_grad = jnp.dot(grad_full, full_weight, preferred_element_type=jnp.float32)
    mixed_grad = mixed_grad.astype(jnp.bfloat16)
    weight_grad = lax.psum_scatter(
        lax.dot_general(
            grad_full, mixed, (((0,), (0,)), ((), ())), preferred_element_type=jnp.float32
        ),
        "ctx",
        scatter_dimension=0,
        tiled=True,
    )
    grad_view = mixed_grad.reshape(tok_dev, groups, head_size)
    delta = jnp.sum(
        grad_view.astype(jnp.float32)
        * mixed.reshape(tok_dev, groups, head_size).astype(jnp.float32),
        axis=2,
    ).T
    band_dots = jnp.einsum(
        "qhd,khd->hqk", grad_view, band_values, preferred_element_type=jnp.float32
    )
    first_dots = jnp.einsum(
        "qhd,khd->hqk", grad_view, first_values, preferred_element_type=jnp.float32
    )
    band_slopes = (band_prob * (band_dots - delta[:, :, None])).astype(jnp.bfloat16)
    first_slopes = (first_prob * (first_dots - delta[:, :, None])).astype(jnp.bfloat16)
    query_sum = jnp.einsum(
        "hqk,khd->qhd", band_slopes, band_keys, preferred_element_type=jnp.float32
    )
    query_sum = query_sum + jnp.einsum(
        "hqk,khd->qhd", first_slopes, first_keys, preferred_element_type=jnp.float32
    )
    query_grad = (query_sum * scale).reshape(tok_dev, features).astype(jnp.bfloat16)
    band_dk = jnp.einsum(
        "hqk,qhd->khd", band_slopes, query_view, preferred_element_type=jnp.float32
    )
    band_dv = jnp.einsum("hqk,qhd->khd", band_low, grad_view, preferred_element_type=jnp.float32)
    partials = jnp.stack(
        [
            band_dk.reshape(band_count, tok_dev, features),
            band_dv.reshape(band_count, tok_dev, features),
        ],
        axis=1,
    )
    first_dk = jnp.einsum(
        "hqk,qhd->khd", first_slopes, query_view, preferred_element_type=jnp.float32
    )
    first_dv = jnp.einsum("hqk,qhd->khd", first_low, grad_view, preferred_element_type=jnp.float32)
    first_part = jnp.stack([first_dk.reshape(block, features), first_dv.reshape(block, features)])
    carried = partials[0]
    for turn in range(1, 2 * reach_runs + 1):
        carried = (
            passed_along(carried.astype(jnp.bfloat16), "ctx", -1).astype(carried.dtype)
            + partials[turn]
        )
    summed = passed_along(carried.astype(jnp.bfloat16), "ctx", reach_runs).astype(carried.dtype)
    first_sum = lax.psum(first_part, "ctx")
    head_rows = summed[:, :block] + jnp.where(run_index == 0, first_sum, jnp.zeros_like(first_sum))
    summed = jnp.concatenate([head_rows, summed[:, block:]], axis=1)
    key_grad = (summed[0] * scale).astype(jnp.bfloat16)
    value_grad = summed[1].astype(jnp.bfloat16)
    return (attended, query_grad, key_grad, value_grad, weight_grad)


def solution(mesh):
    placed = (
        P("ctx", "head"),
        P("ctx", "head"),
        P("ctx", "head"),
        P("ctx", "head"),
        P(),
        P("ctx", "head"),
    )
    return jax.shard_map(
        local,
        mesh=mesh,
        in_specs=placed,
        out_specs=(
            P("ctx", "head"),
            P("ctx", "head"),
            P("ctx", "head"),
            P("ctx", "head"),
            P("ctx", "head"),
        ),
        check_vma=False,
    )
```

profile of v0, /device:TPU:16, one launch (start us, length us, event | category | flops | bytes accessed | tf_op | source)
XLA Modules:
  0.0 1288.9 jit_solution(8840881994418569092)
XLA Ops:
  8.1 1.1 copy.109
  9.2 1.1 copy.110
  12.3 8.1 collective-permute-start
  20.5 11.3 collective-permute-done
  31.7 1.2 collective-permute-start.1
  32.9 18.8 %collective-permute-done.1 = bf16[2,256,512]{1,2,0:T(8,128)(2,1)S(1)} collective-permute-done((bf16[2,256,512]{1,2,0:T(8,128)(2,1)S(1)}, bf16[2,256,512]{1,2,0:T(8,128)(2,1)S(1)}, u32[]{:S(2)}, u32[]{:S(2)}) %collective-permute-start.1) | collective-permute-done | bytes 524320 | tf_op jit(solution)/shard_map/ppermute | solution.py:13
  51.8 2.5 collective-permute-start.2
  54.4 16.7 %collective-permute-done.2 = bf16[2,256,512]{1,2,0:T(8,128)(2,1)S(1)} collective-permute-done((bf16[2,256,512]{1,2,0:T(8,128)(2,1)S(1)}, bf16[2,256,512]{1,2,0:T(8,128)(2,1)S(1)}, u32[]{:S(2)}, u32[]{:S(2)}) %collective-permute-start.2) | collective-permute-done | bytes 524320 | tf_op jit(solution)/shard_map/ppermute | solution.py:13
  71.4 16.7 %collective-permute-done.3 = bf16[2,256,512]{1,2,0:T(8,128)(2,1)S(1)} collective-permute-done((bf16[2,256,512]{1,2,0:T(8,128)(2,1)S(1)}, bf16[2,256,512]{1,2,0:T(8,128)(2,1)S(1)}, u32[]{:S(2)}, u32[]{:S(2)}) %collective-permute-start.3) | collective-permute-done | bytes 524320 | tf_op jit(solution)/shard_map/ppermute | solution.py:13
  88.4 525.0 %all-reduce.3.cloned.1.call-done = bf16[2,128,512]{1,2,0:T(8,128)(2,1)} async-done(((bf16[2,128,512]{1,2,0:T(8,128)(2,1)}), bf16[2,128,512]{1,2,0:T(8,128)(2,1)}) %all-reduce.3.cloned.1.call-update) | async-done | bytes 262160 | tf_op jit(solution)/shard_map/psum | solution.py:18
  613.4 1.6 fusion.41
  615.0 1.1 fusion.43
  616.3 1.2 fusion.40
  617.6 0.9 copy.162
  618.4 1.5 reshape.65
  619.9 2.1 copy.111
  622.0 1.3 reshape_squeeze.12
  623.4 1.1 fusion.42
  625.5 1.2 copy-done.14
  626.7 1.0 fusion.44
  628.6 4.8 convolution_convert_fusion.1
  633.3 1.8 copy.122
  635.1 1.2 fusion.47
  636.4 2.9 multiply_reduce_fusion
  641.5 5.0 convolution_convert_fusion
  646.8 6.1 convolution_bitcast_fusion
  652.9 9.3 copy.160
  662.2 0.9 copy-done.13
  663.1 2.5 convolution_bitcast_fusion.1
  665.6 4.6 reshape.62
  670.2 3.1 copy.137
  673.3 3.9 multiply_convert_fusion
  678.8 6.5 copy.133
  685.3 4.1 stack_reshape.12
  689.4 3.3 copy.136
  692.6 1.3 fusion.32
  693.9 2.3 collective-permute-start.5
  696.2 9.8 collective-permute-done.5
  706.2 4.9 collective-permute-start.6
  711.1 6.9 collective-permute-done.6
  718.1 7.1 collective-permute-start.7
  725.1 9.1 collective-permute-done.7
  734.4 6.8 collective-permute-start.8
  741.2 9.7 collective-permute-done.8
  751.9 0.8 copy.141
  752.7 10.9 collective-permute-done.9
  763.7 514.7 %all-reduce.5.cloned.1.call-done = f32[2,128,512]{1,2,0:T(8,128)} async-done(((f32[2,128,512]{1,2,0:T(8,128)}), f32[2,128,512]{1,2,0:T(8,128)}) %all-reduce.5.cloned.1.call-update) | async-done | bytes 524304 | tf_op jit(solution)/shard_map/psum | solution.py:144
  1278.4 1.1 slice_add_fusion
  (102 shorter events, 12.0 us)
Async XLA Ops:
  8.0 46.2 %copy-start = (s32[128,3]{0,1:T(4,128)S(1)}, s32[128,3]{0,1:T(4,128)}, u32[]{:S(2)}) copy-start(s32[128,3]{0,1:T(4,128)} %param.10) | copy-start | bytes 4612
  8.0 80.2 %copy-start.20 = (bf16[256,512]{1,0:T(8,128)(2,1)S(1)}, bf16[256,512]{1,0:T(8,128)(2,1)}, u32[]{:S(2)}) copy-start(bf16[256,512]{1,0:T(8,128)(2,1)} %param.6) | copy-start | bytes 786436
  8.0 605.4 %all-reduce.3.cloned.1.call-start = ((), (), s32[]{:S(2)}) async-start(), calls=%async_computation.2 | async-start | bytes 524288 | tf_op jit(solution)/shard_map/psum | solution.py:18
  11.1 617.5 %all-gather.5.cloned.1.call-start = ((), (), s32[]{:S(2)}) async-start(), calls=%async_computation.5 | async-start | bytes 2621440 | tf_op jit(solution)/shard_map/all_gather | solution.py:89
  11.6 616.9 %all-gather.3.cloned.1.call-start = ((), (), s32[]{:S(2)}) async-start(), calls=%async_computation.3 | async-start | bytes 4259840 | tf_op jit(solution)/shard_map/all_gather | solution.py:82
  12.2 1266.2 %all-reduce.5.cloned.1.call-start = ((), (), s32[]{:S(2)}) async-start(), calls=%async_computation.6 | async-start | bytes 1048576 | tf_op jit(solution)/shard_map/psum | solution.py:144
  12.3 19.4 %collective-permute-start = (bf16[2,256,512]{1,2,0:T(8,128)(2,1)S(1)}, bf16[2,256,512]{1,2,0:T(8,128)(2,1)S(1)}, u32[]{:S(2)}, u32[]{:S(2)}) collective-permute-start(bf16[2,256,512]{1,2,0:T(8,128)(2,1)S(1)} %pad_maximum_fusion.1), channel_id=1, source_target_pairs={{0,248},{4,252},{8,0},{12,4},{16,8},{20,12},{24,16},{28,20},{32,24... | collective-permute-start | bytes 1572872 | tf_op jit(solution)/shard_map/ppermute | solution.py:13
  31.7 20.0 %collective-permute-start.1 = (bf16[2,256,512]{1,2,0:T(8,128)(2,1)S(1)}, bf16[2,256,512]{1,2,0:T(8,128)(2,1)S(1)}, u32[]{:S(2)}, u32[]{:S(2)}) collective-permute-start(bf16[2,256,512]{1,2,0:T(8,128)(2,1)S(1)} %collective-permute-done), channel_id=1, source_target_pairs={{0,4},{4,8},{8,12},{12,16},{16,20},{20,24},{24,28},{28,32},{32,36}... | collective-permute-start | bytes 1572872 | tf_op jit(solution)/shard_map/ppermute | solution.py:13
  51.8 19.4 %collective-permute-start.2 = (bf16[2,256,512]{1,2,0:T(8,128)(2,1)S(1)}, bf16[2,256,512]{1,2,0:T(8,128)(2,1)S(1)}, u32[]{:S(2)}, u32[]{:S(2)}) collective-permute-start(bf16[2,256,512]{1,2,0:T(8,128)(2,1)S(1)} %collective-permute-done.1), channel_id=1, source_target_pairs={{0,4},{4,8},{8,12},{12,16},{16,20},{20,24},{24,28},{28,32},{32,36}... | collective-permute-start | bytes 1572872 | tf_op jit(solution)/shard_map/ppermute | solution.py:13
  71.1 17.0 %collective-permute-start.3 = (bf16[2,256,512]{1,2,0:T(8,128)(2,1)S(1)}, bf16[2,256,512]{1,2,0:T(8,128)(2,1)S(1)}, u32[]{:S(2)}, u32[]{:S(2)}) collective-permute-start(bf16[2,256,512]{1,2,0:T(8,128)(2,1)S(1)} %collective-permute-done.2), channel_id=1, source_target_pairs={{0,4},{4,8},{8,12},{12,16},{16,20},{20,24},{24,28},{28,32},{32,36}... | collective-permute-start | bytes 1572872 | tf_op jit(solution)/shard_map/ppermute | solution.py:13
  88.2 527.9 %collective-permute-start.4 = (bf16[2,256,512]{1,2,0:T(8,128)(2,1)S(1)}, bf16[2,256,512]{1,2,0:T(8,128)(2,1)S(1)}, u32[]{:S(2)}, u32[]{:S(2)}) collective-permute-start(bf16[2,256,512]{1,2,0:T(8,128)(2,1)S(1)} %collective-permute-done.3), channel_id=1, source_target_pairs={{0,4},{4,8},{8,12},{12,16},{16,20},{20,24},{24,28},{28,32},{32,36}... | collective-permute-start | bytes 1572872 | tf_op jit(solution)/shard_map/ppermute | solution.py:13
  88.4 527.9 %copy-start.8 = (bf16[256,512]{0,1:T(8,128)(2,1)}, bf16[256,512]{0,1:T(8,128)(2,1)S(1)}, u32[]{:S(2)}) copy-start(bf16[256,512]{0,1:T(8,128)(2,1)S(1)} %copy.163) | copy-start | bytes 786436
  619.9 3.5 copy-start.4
  619.9 3.5 copy-start.9
  623.4 1.2 copy-start.11
  624.5 3.2 copy-start.3
  624.7 2.1 copy-start.18
  625.5 1.2 copy-start.14
  636.4 3.0 copy-start.12
  636.4 2.9 copy-start.19
  639.6 0.7 copy-start.16
  641.4 639.9 %reduce-scatter.5.cloned.1.call-start = ((), (), s32[]{:S(2)}) async-start(), calls=%async_computation.4 | async-start | bytes 2621440 | tf_op jit(solution)/shard_map/reduce_scatter | solution.py:86
  641.5 5.3 copy-start.15
  646.5 634.8 %reduce-scatter.7.cloned.1.call-start = ((), (), s32[]{:S(2)}) async-start(), calls=%async_computation.7 | async-start | bytes 8519680
  662.2 0.9 copy-start.13
  670.2 3.1 copy-start.10
  677.2 1.6 copy-start.6
  692.6 13.4 %copy-start.2 = (f32[5,1,256,512]{2,3,1,0:T(8,128)S(1)}, f32[5,1,256,512]{2,3,1,0:T(8,128)}, u32[]{:S(2)}) copy-start(f32[5,1,256,512]{2,3,1,0:T(8,128)} %copy.136) | copy-start | bytes 7864324
  693.9 12.1 collective-permute-start.5
  706.2 11.7 collective-permute-start.6
  718.1 16.2 %collective-permute-start.7 = (bf16[2,256,512]{1,2,0:T(8,128)(2,1)S(1)}, bf16[2,256,512]{1,2,0:T(8,128)(2,1)S(1)}, u32[]{:S(2)}, u32[]{:S(2)}) collective-permute-start(bf16[2,256,512]{1,2,0:T(8,128)(2,1)S(1)} %fusion.24), channel_id=1, source_target_pairs={{0,252},{4,0},{8,4},{12,8},{16,12},{20,16},{24,20},{28,24},{32,28}... | collective-permute-start | bytes 1572872 | tf_op jit(solution)/shard_map/ppermute | solution.py:13
  734.4 16.7 %copy-start.17 = (bf16[4,256,128]{1,2,0:T(8,128)(2,1)S(1)}, bf16[4,256,128]{1,2,0:T(8,128)(2,1)}, u32[]{:S(2)}) copy-start(bf16[4,256,128]{1,2,0:T(8,128)(2,1)} %copy-done.16) | copy-start | bytes 786436
  734.4 16.9 %copy-start.5 = (bf16[1280,4,128]{0,2,1:T(8,128)(2,1)S(1)}, bf16[1280,4,128]{0,2,1:T(8,128)(2,1)}, u32[]{:S(2)}) copy-start(bf16[1280,4,128]{0,2,1:T(8,128)(2,1)} %copy-done.4) | copy-start | bytes 3932164
  734.4 16.9 %copy-start.7 = (bf16[4,256,1280]{1,2,0:T(8,128)(2,1)S(1)}, bf16[4,256,1280]{1,2,0:T(8,128)(2,1)}, u32[]{:S(2)}) copy-start(bf16[4,256,1280]{1,2,0:T(8,128)(2,1)} %copy-done.6) | copy-start | bytes 7864324
  734.4 16.5 %collective-permute-start.8 = (bf16[2,256,512]{1,2,0:T(8,128)(2,1)S(1)}, bf16[2,256,512]{1,2,0:T(8,128)(2,1)S(1)}, u32[]{:S(2)}, u32[]{:S(2)}) collective-permute-start(bf16[2,256,512]{1,2,0:T(8,128)(2,1)S(1)} %fusion.14), channel_id=1, source_target_pairs={{0,252},{4,0},{8,4},{12,8},{16,12},{20,16},{24,20},{28,24},{32,28}... | collective-permute-start | bytes 1572872 | tf_op jit(solution)/shard_map/ppermute | solution.py:13
  751.0 12.6 collective-permute-start.9
  763.6 517.7 %copy-start.1 = (s32[128,3]{0,1:T(4,128)S(1)}, s32[128,3]{0,1:T(4,128)}, u32[]{:S(2)}) copy-start(s32[128,3]{0,1:T(4,128)} %param.10) | copy-start | bytes 4612
Sparse Core Ops, SparseCore 0:
  12.0 601.3 all-reduce.2
  641.6 636.8 all-reduce.4
Sparse Core Ops, SparseCore 1:
  13.4 37.5 all-gather.4
  52.6 333.4 all-gather.2
  646.6 43.9 reduce-scatter.4
  693.6 356.1 reduce-scatter.6
where the time goes:
time: 1290 us
  waiting for transfers between devices  1150 us (89%)
  local copies, waits for them, and re-layouts  50.4 us (4%)
  starting transfers between devices  33.4 us (3%)
  matrix products  31.6 us (2%)
  between operations  16.2 us (1%)
    psum x1, waiting for transfers between devices, spread(): return lax.psum(kept, axis)  525 us
    psum x1, waiting for transfers between devices, local(): first_sum = lax.psum(first_part, 'ctx')  515 us
    ppermute x10, waiting for transfers between devices, passed_along(): return lax.ppermute(x, axis, [(i, (i + by) % peers) for i in range(peers)])  110 us
    ppermute x10, starting transfers between devices, passed_along(): return lax.ppermute(x, axis, [(i, (i + by) % peers) for i in range(peers)])  33 us
  transfers between devices with their start and end apart: 16, of which 11 were waited for; matrix products, arithmetic and copies ran while one was open for 5% of the time, Pallas kernels for 0%

commit v1 on v0

--- a/solution.py
+++ b/solution.py
@@ -15,7 +15,7 @@
 
 def spread(value, axis, source):
     kept = jnp.where(lax.axis_index(axis) == source, value, 0).astype(value.dtype)
-    return lax.psum(kept, axis)
+    return jnp.sum(lax.all_gather(kept, axis), axis=0)
 
 
 def local(queries, key_heads, value_heads, out_weight, block_lists, out_grad):

time: 1290 us -> 1780 us (1.38)
  waiting for transfers between devices: 1150 us -> 1630 us
  other arithmetic: 6.55 us -> 24.5 us
    psum x1 -> x0, waiting for transfers between devices: 525 us -> none  [spread(): return lax.psum(kept, axis)]
    all_gather x0 -> x1, waiting for transfers between devices: none -> 365 us  [spread(): return jnp.sum(lax.all_gather(kept, axis), axis=0)]
    unnamed x7, waiting for transfers between devices: 1.12 us -> 342 us
    all_gather x1, waiting for transfers between devices: 0.02 us -> 259 us  [local(): full_weight = lax.all_gather(out_weight, 'ctx', axis=0, tiled=True)]
    reduce_scatter x1, waiting for transfers between devices: 0.01 us -> 38.2 us  [local(): lax.psum_scatter(partial_out.astype(jnp.bfloat16), 'head', scatter_dimens...]
  transfers between devices with their start and end apart: 16 -> 16, of which waited for: 11 -> 15; matrix products, arithmetic and copies ran while one was open for 5% -> 4% of each run, Pallas kernels for 0% -> 0%
where the time goes in v1:
time: 1780 us
  waiting for transfers between devices  1630 us (92%)
  local copies, waits for them, and re-layouts  45.7 us (3%)
  starting transfers between devices  38 us (2%)
  matrix products  35.1 us (2%)
  other arithmetic  24.5 us (1%)
    psum x1, waiting for transfers between devices, local(): first_sum = lax.psum(first_part, 'ctx')  503 us
    all_gather x1, waiting for transfers between devices, spread(): return jnp.sum(lax.all_gather(kept, axis), axis=0)  365 us
    unnamed x7, waiting for transfers between devices  342 us
    all_gather x1, waiting for transfers between devices, local(): full_weight = lax.all_gather(out_weight, 'ctx', axis=0, tiled=True)  259 us
    ppermute x10, waiting for transfers between devices, passed_along(): return lax.ppermute(x, axis, [(i, (i + by) % peers) for i in range(peers)])  117 us
    reduce_scatter x1, waiting for transfers between devices, local(): lax.psum_scatter(partial_out.astype(jnp.bfloat16), 'head', scatter_dimens...  38.2 us
    ppermute x10, starting transfers between devices, passed_along(): return lax.ppermute(x, axis, [(i, (i + by) % peers) for i in range(peers)])  37.6 us
  transfers between devices with their start and end apart: 16, of which 15 were waited for; matrix products, arithmetic and copies ran while one was open for 4% of the time, Pallas kernels for 0%

profile of v1, /device:TPU:16, one launch (start us, length us, event | category | flops | bytes accessed | tf_op | source)
XLA Modules:
  0.0 1782.9 jit_solution(18125605261347129518)
XLA Ops:
  8.7 1.7 fusion.29
  11.6 8.1 collective-permute-start
  19.7 11.2 collective-permute-done
  30.9 1.3 collective-permute-start.1
  32.2 16.4 collective-permute-done.1
  48.6 1.9 collective-permute-start.2
  50.5 16.6 collective-permute-done.2
  67.5 17.6 collective-permute-done.3
  85.5 16.8 collective-permute-done.4
  102.6 1.3 reshape_squeeze.13
  103.9 2.6 copy.121
  106.6 1.5 reshape_squeeze.12
  108.1 3.4 fusion.34
  111.6 259.4 %all-gather.5.cloned.1.call-done = bf16[4096,512]{1,0:T(8,128)(2,1)} async-done(((bf16[64,512]{1,0:T(8,128)(2,1)}), bf16[4096,512]{1,0:T(8,128)(2,1)}) %all-gather.5.cloned.1.call-update) | async-done | bytes 4194320 | tf_op jit(solution)/shard_map/all_gather | solution.py:82
  371.0 4.1 convolution_convert_fusion.1
  375.9 364.9 %all-gather.9.cloned.1.call-done = bf16[128,128,512]{2,1,0:T(8,128)(2,1)} async-done(((bf16[2,128,512]{2,1,0:T(8,128)(2,1)}), bf16[128,128,512]{2,1,0:T(8,128)(2,1)}) %all-gather.9.cloned.1.call-update) | async-done | bytes 16777232 | tf_op jit(solution)/shard_map/all_gather | solution.py:18
  740.7 8.9 reduce_sum.39
  750.7 3.2 fusion.1
  754.8 3.3 fusion.2
  758.0 1.7 copy.115
  759.7 1.2 fusion.36
  760.9 2.0 fusion.39
  762.9 2.8 multiply_reduce_fusion
  766.7 1.8 copy.139
  768.5 1.2 fusion.38
  770.5 1.9 pad_maximum_fusion.2
  772.7 4.8 convolution_convert_fusion
  777.6 6.1 convolution_bitcast_fusion
  783.7 9.1 copy.155
  793.7 4.2 multiply_convert_fusion
  799.5 6.5 copy.128
  806.0 4.1 stack_reshape.12
  810.1 2.5 convolution_bitcast_fusion.1
  812.6 4.2 copy.130
  816.7 4.3 stack_reshape.13
  821.3 1.5 copy-done.7
  823.2 5.3 collective-permute-start.5
  829.1 7.3 collective-permute-done.5
  836.6 7.1 collective-permute-start.6
  843.7 7.0 collective-permute-done.6
  850.9 6.9 collective-permute-start.7
  857.8 6.8 collective-permute-done.7
  864.8 6.9 collective-permute-start.8
  871.7 6.8 collective-permute-done.8
  880.4 10.9 collective-permute-done.9
  891.5 502.8 %all-reduce.2.cloned.1.call-done = f32[2,128,512]{2,1,0:T(8,128)} async-done(((f32[2,128,512]{2,1,0:T(8,128)}), f32[2,128,512]{2,1,0:T(8,128)}) %all-reduce.2.cloned.1.call-update) | async-done | bytes 524304 | tf_op jit(solution)/shard_map/psum | solution.py:144
  1396.9 38.2 %reduce-scatter.5.cloned.1.call-done = bf16[256,1024]{1,0:T(8,128)(2,1)} async-done(((bf16[256,4096]{1,0:T(8,128)(2,1)}), bf16[256,1024]{1,0:T(8,128)(2,1)}) %reduce-scatter.5.cloned.1.call-update) | async-done | bytes 524304 | tf_op jit(solution)/shard_map/reduce_scatter | solution.py:86
  1435.1 341.0 %reduce-scatter.7.cloned.1.call-done = f32[64,512]{1,0:T(8,128)} async-done(((f32[4096,512]{1,0:T(8,128)}), f32[64,512]{1,0:T(8,128)}) %reduce-scatter.7.cloned.1.call-update) | async-done | bytes 131088
  (90 shorter events, 17.7 us)
Async XLA Ops:
  7.2 60.1 %copy-start = (s32[128,3]{0,1:T(4,128)S(1)}, s32[128,3]{0,1:T(4,128)}, u32[]{:S(2)}) copy-start(s32[128,3]{0,1:T(4,128)} %param.10) | copy-start | bytes 4612
  7.2 59.9 %copy-start.13 = (bf16[256,512]{1,0:T(8,128)(2,1)S(1)}, bf16[256,512]{1,0:T(8,128)(2,1)}, u32[]{:S(2)}) copy-start(bf16[256,512]{1,0:T(8,128)(2,1)} %param.6) | copy-start | bytes 786436
  7.2 104.4 %all-gather.7.cloned.1.call-start = ((), (), s32[]{:S(2)}) async-start(), calls=%async_computation.4 | async-start | bytes 2621440 | tf_op jit(solution)/shard_map/all_gather | solution.py:89
  7.9 363.0 %all-gather.5.cloned.1.call-start = ((), (), s32[]{:S(2)}) async-start(), calls=%async_computation.2 | async-start | bytes 4259840 | tf_op jit(solution)/shard_map/all_gather | solution.py:82
  8.7 732.1 %all-gather.9.cloned.1.call-start = ((), (), s32[]{:S(2)}) async-start(), calls=%async_computation.6 | async-start | bytes 17039360 | tf_op jit(solution)/shard_map/all_gather | solution.py:18
  10.5 1383.8 %all-reduce.2.cloned.1.call-start = ((), (), s32[]{:S(2)}) async-start(), calls=%async_computation.5 | async-start | bytes 1048576 | tf_op jit(solution)/shard_map/psum | solution.py:144
  11.6 19.3 %collective-permute-start = (bf16[2,256,512]{2,1,0:T(8,128)(2,1)S(1)}, bf16[2,256,512]{2,1,0:T(8,128)(2,1)S(1)}, u32[]{:S(2)}, u32[]{:S(2)}) collective-permute-start(bf16[2,256,512]{2,1,0:T(8,128)(2,1)S(1)} %pad_maximum_fusion), channel_id=1, source_target_pairs={{0,248},{4,252},{8,0},{12,4},{16,8},{20,12},{24,16},{28,20},{32,24... | collective-permute-start | bytes 1572872 | tf_op jit(solution)/shard_map/ppermute | solution.py:13
  30.9 17.7 collective-permute-start.1
  48.6 18.5 %collective-permute-start.2 = (bf16[2,256,512]{2,1,0:T(8,128)(2,1)S(1)}, bf16[2,256,512]{2,1,0:T(8,128)(2,1)S(1)}, u32[]{:S(2)}, u32[]{:S(2)}) collective-permute-start(bf16[2,256,512]{2,1,0:T(8,128)(2,1)S(1)} %collective-permute-done.1), channel_id=1, source_target_pairs={{0,4},{4,8},{8,12},{12,16},{16,20},{20,24},{24,28},{28,32},{32,36}... | collective-permute-start | bytes 1572872 | tf_op jit(solution)/shard_map/ppermute | solution.py:13
  67.1 18.0 %collective-permute-start.3 = (bf16[2,256,512]{2,1,0:T(8,128)(2,1)S(1)}, bf16[2,256,512]{2,1,0:T(8,128)(2,1)S(1)}, u32[]{:S(2)}, u32[]{:S(2)}) collective-permute-start(bf16[2,256,512]{2,1,0:T(8,128)(2,1)S(1)} %collective-permute-done.2), channel_id=1, source_target_pairs={{0,4},{4,8},{8,12},{12,16},{16,20},{20,24},{24,28},{28,32},{32,36}... | collective-permute-start | bytes 1572872 | tf_op jit(solution)/shard_map/ppermute | solution.py:13
  85.1 17.1 collective-permute-start.4
  106.6 5.0 copy-start.2
  762.9 2.8 copy-start.8
  762.9 2.8 copy-start.12
  766.7 6.0 copy-start.10
  772.4 662.6 %reduce-scatter.5.cloned.1.call-start = ((), (), s32[]{:S(2)}) async-start(), calls=%async_computation.3 | async-start | bytes 2621440 | tf_op jit(solution)/shard_map/reduce_scatter | solution.py:86
  777.5 998.5 %reduce-scatter.7.cloned.1.call-start = ((), (), s32[]{:S(2)}) async-start(), calls=%async_computation.7 | async-start | bytes 8519680
  792.7 1.0 copy-start.9
  797.9 1.6 copy-start.4
  816.7 4.3 copy-start.6
  821.0 1.8 copy-start.7
  823.2 13.2 collective-permute-start.5
  836.6 14.1 collective-permute-start.6
  850.9 27.9 %copy-start.11 = (bf16[4,256,128]{1,2,0:T(8,128)(2,1)S(1)}, bf16[4,256,128]{1,2,0:T(8,128)(2,1)}, u32[]{:S(2)}) copy-start(bf16[4,256,128]{1,2,0:T(8,128)(2,1)} %fusion.6) | copy-start | bytes 786436
  850.9 28.1 %copy-start.3 = (bf16[1280,4,128]{0,2,1:T(8,128)(2,1)S(1)}, bf16[1280,4,128]{0,2,1:T(8,128)(2,1)}, u32[]{:S(2)}) copy-start(bf16[1280,4,128]{0,2,1:T(8,128)(2,1)} %copy-done.2) | copy-start | bytes 3932164
  850.9 28.1 %copy-start.5 = (bf16[4,256,1280]{1,2,0:T(8,128)(2,1)S(1)}, bf16[4,256,1280]{1,2,0:T(8,128)(2,1)}, u32[]{:S(2)}) copy-start(bf16[4,256,1280]{1,2,0:T(8,128)(2,1)} %copy-done.4) | copy-start | bytes 7864324
  850.9 13.7 collective-permute-start.7
  864.8 13.7 collective-permute-start.8
  878.7 12.6 collective-permute-start.9
  891.3 884.8 %copy-start.1 = (s32[128,3]{0,1:T(4,128)S(1)}, s32[128,3]{0,1:T(4,128)}, u32[]{:S(2)}) copy-start(s32[128,3]{0,1:T(4,128)} %param.10) | copy-start | bytes 4612
Sparse Core Ops, SparseCore 0:
  9.8 34.5 all-gather.6
  46.2 324.6 all-gather.4
  373.3 367.3 all-gather.8
  772.6 621.6 all-reduce.1
  1397.4 37.6 reduce-scatter.4
  1438.0 337.9 reduce-scatter.6
